TPU v7x, 128 devices: a whole 4x4x4 slice. The times are simulated.
128 devices in a mesh: section: 4 (over y), dp: 2 (over core), expert: 16 (over x, z).
Axes of the slice: x: 4, y: 4, z: 4, core: 2. Of those that a mesh axis runs over, the one named last changes fastest.
Arguments:
- stashed: bfloat16 [4, 6144, 2048], P('section', ('dp', 'expert')), may hold values from -6 to 6
- expert_ids: int32 [4, 6144, 8], P('section', ('dp', 'expert')), may hold values from 0 to 63, all different within a row; in each aligned block of 192 rows (0 to 191, 192 to 383, ..., all dimensions but the last counted through in order) at most 48 rows name the same one
- route_probs: float32 [4, 6144, 8], P('section', ('dp', 'expert')), may hold values from 0.02 to 1
- w_gate: bfloat16 [4, 64, 2048, 768], P('section', ('dp', 'expert')), may hold values from -0.125 to 0.125
- w_up: bfloat16 [4, 64, 2048, 768], P('section', ('dp', 'expert')), may hold values from -0.125 to 0.125
- w_down: bfloat16 [4, 64, 768, 2048], P('section', ('dp', 'expert')), may hold values from -0.21875 to 0.21875
Outputs:
- handed: bfloat16 [4, 6144, 2048], P('section', ('dp', 'expert'))
- balance: float32 [4], P('section')
Inputs may be any that keep to these rules, and one draw needn't show every extreme that they name: `expert_ids`: each token names 8 different experts; among the tokens of one device (aligned blocks of 192 tokens) no expert is named more than 48 times, and in every draw some expert is named exactly 48 times in some block.
All inputs are finite; a program needn't handle non-finite values.
Results may differ from a plain program's by a relative error of at most 0.0032.
Values may be sent and summed in bfloat16 or wider, within the bound.
No kernel may reach another device: no remote copies, remote signals or barrier semaphores. Data moves between devices by JAX's collectives and lax.ppermute only.
A program may use at most 128 MiB of HBM per device.

v0:
```python
import jax
import jax.numpy as jnp
from jax import lax
from jax.sharding import PartitionSpec as P


def passed_along(value, axis, steps):
    count = lax.axis_size(axis)
    pairs = [(source, (source + steps) % count) for source in range(count)]
    return lax.ppermute(value, axis, pairs)


def expert_rows(received, gate_w, up_w, down_w, form_in, form_out):
    gate_act = jnp.einsum(form_in, received, gate_w, preferred_element_type=jnp.float32)
    up_act = jnp.einsum(form_in, received, up_w, preferred_element_type=jnp.float32)
    hidden = (jax.nn.silu(gate_act) * up_act).astype(jnp.bfloat16)
    return jnp.einsum(form_out, hidden, down_w, preferred_element_type=jnp.float32).astype(
        jnp.bfloat16
    )


def per_device(stashed, expert_ids, route_probs, w_gate, w_up, w_down):
    tokens_in = stashed[0]
    choice_ids = expert_ids[0]
    probs = route_probs[0]
    gate_w = w_gate[0]
    up_w = w_up[0]
    down_w = w_down[0]
    expert_count = lax.axis_size("expert")
    dp_count = lax.axis_size("dp")
    local_count = gate_w.shape[0]
    all_experts = dp_count * expert_count * local_count
    token_count, top_count = choice_ids.shape
    model_width = tokens_in.shape[1]
    capacity = 2 * token_count * top_count // all_experts
    inputs = tokens_in.astype(jnp.float32)
    normed = (inputs * lax.rsqrt(jnp.mean(inputs * inputs, axis=-1, keepdims=True) + 1e-06)).astype(
        jnp.bfloat16
    )
    flat_ids = choice_ids.reshape(-1)
    labels = jnp.arange(all_experts, dtype=jnp.int32)
    onehot = (flat_ids[:, None] == labels[None, :]).astype(jnp.int32)
    running = jnp.cumsum(onehot, axis=0)
    position = jnp.sum(running * onehot, axis=1) - 1
    slot_rows = flat_ids * capacity + position
    sent_rows = (
        jnp.zeros((all_experts * capacity, model_width), jnp.bfloat16)
        .at[slot_rows]
        .set(jnp.repeat(normed, top_count, axis=0))
    )
    arranged = sent_rows.reshape(dp_count * expert_count, local_count, capacity, model_width)
    received = lax.all_to_all(arranged, ("dp", "expert"), split_axis=0, concat_axis=0, tiled=True)
    result = expert_rows(received, gate_w, up_w, down_w, "secd,edf->secf", "secf,efd->secd")
    returned = lax.all_to_all(result, ("dp", "expert"), split_axis=0, concat_axis=0, tiled=True)
    picked = returned.reshape(all_experts * capacity, model_width)[slot_rows]
    picked = picked.reshape(token_count, top_count, model_width).astype(jnp.float32)
    weights = probs / jnp.sum(probs, axis=-1, keepdims=True)
    mixture = jnp.sum(weights[:, :, None] * picked, axis=1)
    layer_out = (inputs + mixture).astype(jnp.bfloat16)
    counts = jnp.sum(onehot, axis=0).astype(jnp.float32)
    mass = jnp.dot(weights.reshape(-1), onehot.astype(jnp.float32), precision=lax.Precision.HIGHEST)
    counts_all, mass_all = lax.psum((counts, mass), ("dp", "expert"))
    tokens_all = token_count * dp_count * expert_count
    loss = all_experts * jnp.sum(counts_all / (tokens_all * top_count) * (mass_all / tokens_all))
    handed = passed_along(layer_out, "section", 1)
    return (handed[None], loss.reshape(1))


def solution(mesh):
    placed = (
        P("section", ("dp", "expert"), None),
        P("section", ("dp", "expert"), None),
        P("section", ("dp", "expert"), None),
        P("section", ("dp", "expert"), None, None),
        P("section", ("dp", "expert"), None, None),
        P("section", ("dp", "expert"), None, None),
    )
    return jax.shard_map(
        per_device,
        mesh=mesh,
        in_specs=placed,
        out_specs=(P("section", ("dp", "expert"), None), P("section")),
        check_vma=False,
    )
```

profile of v0, /device:TPU:2, one launch (start us, length us, event | category | flops | bytes accessed | tf_op | source)
XLA Modules:
  0.0 558.4 jit_solution(3848793365307210415)
XLA Ops:
  0.6 0.8 copy.21
  1.4 0.1 eq.29
  1.5 0.1 eq.25
  1.7 0.7 broadcast_multiply_fusion
  2.4 18.1 %reduce-window.6 = s32[64,12,128]{2,1,0:T(8,128)S(1)} reduce-window(s32[64,12,128]{2,1,0:T(8,128)S(1)} %fusion.29, s32[]{:T(128)} %constant.9.clone.1), window={size=1x1x128 pad=0_0x0_0x127_0}, to_apply=%region_1.0 | reduce-window | flops 12484608 | bytes 786436 | tf_op jit(solution)/shard_map/reduce-window
  20.5 0.2 slice.10
  20.7 0.3 copy.23
  21.1 0.2 broadcast_add_fusion
  21.3 0.2 convert_reduce_fusion
  21.6 0.1 copy.20
  21.7 0.1 mul.51
  21.8 1.4 fusion.26
  23.2 1.3 fusion.27
  24.5 16.3 %scatter_custom_fusion = bf16[3072,2048]{1,0:T(8,128)(2,1)} fusion(s32[1536]{0:T(1024)S(1)} %fusion.33, bf16[]{:T(256)} %constant.8.clone.1, bf16[192,2048]{1,0:T(8,128)(2,1)S(1)} %fusion.27), kind=kCustom, calls=%fused_computation.19 | custom fusion | bytes 13369346 | tf_op jit(solution)/shard_map/scatter | solution.py:49
  40.9 149.1 %all_to_all.10 = bf16[32,2,48,2048]{3,2,1,0:T(8,128)(2,1)S(1)} all-to-all(bf16[32,2,48,2048]{3,2,1,0:T(8,128)(2,1)} %bitcast.78), channel_id=1, replica_groups=mesh['section'=4,'dp'=2,'expert'=16] {'dp','expert'}, dimensions={0} | all-to-all | bytes 25165824 | tf_op jit(solution)/shard_map/all_to_all | solution.py:52
  189.9 4.5 copy-done
  194.4 14.1 %fusion.1 = f32[2,32,48,768]{3,2,1,0:T(8,128)} fusion(bf16[32,2,48,2048]{3,2,1,0:T(8,128)(2,1)S(1)} %all_to_all.10, bf16[1,2,2048,768]{3,2,1,0:T(8,128)(2,1)} %param.10), kind=kOutput, calls=%fused_computation.5 | convolution fusion | flops 9663676416 | bytes 28311552 | tf_op jit(solution)/shard_map/secd,edf->secf/dot_general | solution.py:15
  208.4 29.3 %convert_bitcast_fusion = bf16[32,2,48,2048]{3,2,0,1:T(8,128)(2,1)} fusion(bf16[1,2,768,2048]{3,2,1,0:T(8,128)(2,1)} %param.11, f32[2,32,48,768]{3,2,1,0:T(8,128)} %fusion.1, bf16[32,2,48,2048]{3,2,1,0:T(8,128)(2,1)} %copy-done, bf16[1,2,2048,768]{3,2,1,0:T(8,128)(2,1)} %param.9), kind=kOutput, calls=%fused_computation.4 | convolution fusion | flops 19347800064 | bytes 47185920 | tf_op jit(solution)/shard_map/secf,efd->secd/dot_general | solution.py:17
  237.8 10.8 %copy.27 = bf16[32,2,48,2048]{3,2,1,0:T(8,128)(2,1)} copy(bf16[32,2,48,2048]{3,2,0,1:T(8,128)(2,1)} %convert_bitcast_fusion) | data formatting | bytes 25165824 | tf_op jit(solution)/shard_map/convert_element_type | solution.py:17
  248.6 5.4 all-to-all-start.1
  254.1 0.1 copy.19
  254.2 194.4 %all-to-all-done.1 = bf16[32,2,48,2048]{3,2,1,0:T(8,128)(2,1)} async-done(((bf16[32,2,48,2048]{3,2,1,0:T(8,128)(2,1)}), bf16[32,2,48,2048]{3,2,1,0:T(8,128)(2,1)}, u32[]{:S(2)}, u32[]{:S(2)}) %all-to-all-start.1) | async-done | bytes 12582944 | tf_op jit(solution)/shard_map/all_to_all | solution.py:54
  448.6 19.0 %gather_fusion = bf16[1536,2048]{1,0:T(8,128)(2,1)} fusion(bf16[3072,2048]{1,0:T(8,128)(2,1)} %bitcast.19, s32[2048]{0:T(1024)S(1)} %pad_clamp_fusion), kind=kCustom, calls=%fused_computation | custom fusion | bytes 12589056 | tf_op jit(solution)/shard_map/gather | solution.py:55
  467.6 9.2 %fusion = f32[192,2048]{1,0:T(8,128)S(1)} fusion(bf16[1536,2048]{1,0:T(8,128)(2,1)} %gather_fusion, f32[192,8]{1,0:T(8,128)S(1)} %copy.19), kind=kLoop, calls=%fused_computation.3 | loop fusion | flops 9043968 | bytes 7870464 | tf_op jit(solution)/shard_map/reduce_sum | solution.py:58
  476.9 0.2 fusion.28
  477.1 1.7 collective-permute-start
  478.7 0.1 copy.28
  478.9 0.1 div.46
  479.2 0.4 convolution_bitcast_fusion
  479.6 75.5 %all-reduce = (f32[64]{0:T(128)S(1)}, f32[64]{0:T(128)S(1)}) all-reduce(f32[64]{0:T(128)S(1)} %convolution_bitcast_fusion, f32[64]{0:T(128)S(1)} %convert_element_type.51), channel_id=1, replica_groups=mesh['section'=4,'dp'=2,'expert'=16] {'dp','expert'}, use_global_device_ids=true, to_apply=%region_9.10 | all-reduce | flops 128 | bytes 1024 | tf_op jit(solution)/shard_map/psum | solution.py:62
  555.1 0.6 multiply_reduce_fusion
  556.4 0.9 copy.44
  (20 shorter events, 0.4 us)
Async XLA Ops:
  189.9 4.5 copy-start
  248.6 5.5 copy-start.2
  248.6 200.0 %all-to-all-start.1 = ((bf16[32,2,48,2048]{3,2,1,0:T(8,128)(2,1)}), bf16[32,2,48,2048]{3,2,1,0:T(8,128)(2,1)}, u32[]{:S(2)}, u32[]{:S(2)}) async-start(bf16[32,2,48,2048]{3,2,1,0:T(8,128)(2,1)} %copy.27), calls=%async_computation.1 | async-start | bytes 25165824 | tf_op jit(solution)/shard_map/all_to_all | solution.py:54
  448.6 28.2 %copy-start.1 = (bf16[1,192,2048]{2,1,0:T(8,128)(2,1)S(1)}, bf16[1,192,2048]{2,1,0:T(8,128)(2,1)}, u32[]{:S(2)}) copy-start(bf16[1,192,2048]{2,1,0:T(8,128)(2,1)} %param.6) | copy-start | bytes 2359300
  477.1 79.3 %collective-permute-start = (bf16[192,2048]{1,0:T(8,128)(2,1)S(1)}, bf16[192,2048]{1,0:T(8,128)(2,1)S(1)}, u32[]{:S(2)}, u32[]{:S(2)}) collective-permute-start(bf16[192,2048]{1,0:T(8,128)(2,1)S(1)} %fusion.28), channel_id=1, source_target_pairs={{0,32},{32,64},{64,96},{96,0},{1,33},{33,65},{65,97},{97,1},{2,34}... | collective-permute-start | bytes 2359304 | tf_op jit(solution)/shard_map/ppermute | solution.py:10
where the time goes:
time: 559 us; the launch traced here: 558 us
  blocking collectives  225 us (40%)
  waiting for transfers between devices  194 us (35%)
  local copies, waits for them, and re-layouts  53.8 us (10%)
  matrix products  43.8 us (8%)
  other arithmetic  32.1 us (6%)
  starting transfers between devices  7.09 us (1%)
    all_to_all x1, waiting for transfers between devices, per_device(): lax.all_to_all(result, ('dp', 'expert'), split_axis=0, concat_axis=0, til...  194 us
    all_to_all x1, blocking collectives, per_device(): lax.all_to_all(arranged, ('dp', 'expert'), split_axis=0, concat_axis=0, t...  149 us
    psum x1, blocking collectives, per_device(): counts_all, mass_all = lax.psum((counts, mass), ('dp', 'expert'))  75.5 us
    dot_general x1, matrix products, expert_rows(): jnp.einsum(form_out, hidden, down_w, preferred_element_type=jnp.float32)  29.3 us
    gather x1, local copies, waits for them, and re-layouts, per_device(): picked = returned.reshape(all_experts * capacity, model_width)[slot_rows]  19 us
    another operation x3, other arithmetic  18.4 us
    scatter x1, local copies, waits for them, and re-layouts, per_device(): sent_rows = jnp.zeros((all_experts * capacity, model_width), jnp.bfloat16...  16.3 us
    dot_general x1, matrix products, expert_rows(): jnp.einsum(form_in, received, up_w, preferred_element_type=jnp.float32)  14.1 us
  transfers between devices with their start and end apart: 2, of which 1 were waited for; matrix products, arithmetic and copies ran while one was open for 0% of the time, Pallas kernels for 0%

commit v1 on v0

--- a/solution.py
+++ b/solution.py
@@ -2,6 +2,11 @@
 import jax.numpy as jnp
 from jax import lax
 from jax.sharding import PartitionSpec as P
+from jax.lax import psum
+
+
+def guide_routes_all(arr, net_axis, mesh_name):
+    return psum(psum(arr, net_axis), mesh_name)
 
 
 def passed_along(value, axis, steps):
@@ -59,7 +64,7 @@
     layer_out = (inputs + mixture).astype(jnp.bfloat16)
     counts = jnp.sum(onehot, axis=0).astype(jnp.float32)
     mass = jnp.dot(weights.reshape(-1), onehot.astype(jnp.float32), precision=lax.Precision.HIGHEST)
-    counts_all, mass_all = lax.psum((counts, mass), ("dp", "expert"))
+    counts_all, mass_all = guide_routes_all((counts, mass), "dp", "expert")
     tokens_all = token_count * dp_count * expert_count
     loss = all_experts * jnp.sum(counts_all / (tokens_all * top_count) * (mass_all / tokens_all))
     handed = passed_along(layer_out, "section", 1)

time: 559 us -> 533 us (0.953)
  blocking collectives: 225 us -> 198 us
    psum x1 -> x2, blocking collectives: 75.5 us -> 48.6 us  [guide_routes_all(): return psum(psum(arr, net_axis), mesh_name)]
where the time goes in v1:
time: 533 us; the launch traced here: 531 us
  blocking collectives  198 us (37%)
  waiting for transfers between devices  194 us (36%)
  local copies, waits for them, and re-layouts  53.8 us (10%)
  matrix products  43.8 us (8%)
  other arithmetic  32.1 us (6%)
  starting transfers between devices  7.09 us (1%)
    all_to_all x1, waiting for transfers between devices, per_device(): lax.all_to_all(result, ('dp', 'expert'), split_axis=0, concat_axis=0, til...  194 us
    all_to_all x1, blocking collectives, per_device(): lax.all_to_all(arranged, ('dp', 'expert'), split_axis=0, concat_axis=0, t...  149 us
    psum x2, blocking collectives, guide_routes_all(): return psum(psum(arr, net_axis), mesh_name)  48.6 us
    dot_general x1, matrix products, expert_rows(): jnp.einsum(form_out, hidden, down_w, preferred_element_type=jnp.float32)  29.3 us
    gather x1, local copies, waits for them, and re-layouts, per_device(): picked = returned.reshape(all_experts * capacity, model_width)[slot_rows]  19 us
    another operation x3, other arithmetic  18.4 us
    scatter x1, local copies, waits for them, and re-layouts, per_device(): sent_rows = jnp.zeros((all_experts * capacity, model_width), jnp.bfloat16...  16.3 us
    dot_general x1, matrix products, expert_rows(): jnp.einsum(form_in, received, up_w, preferred_element_type=jnp.float32)  14.1 us
  transfers between devices with their start and end apart: 2, of which 1 were waited for; matrix products, arithmetic and copies ran while one was open for 0% of the time, Pallas kernels for 0%

profile of v1, /device:TPU:2, one launch (start us, length us, event | category | flops | bytes accessed | tf_op | source)
XLA Modules:
  0.0 531.5 jit_solution(830386422751429436)
XLA Ops:
  0.6 0.8 copy.21
  1.4 0.1 eq.29
  1.7 0.7 broadcast_multiply_fusion
  2.4 18.1 %reduce-window.6 = s32[64,12,128]{2,1,0:T(8,128)S(1)} reduce-window(s32[64,12,128]{2,1,0:T(8,128)S(1)} %fusion.29, s32[]{:T(128)} %constant.9.clone.1), window={size=1x1x128 pad=0_0x0_0x127_0}, to_apply=%region_1.0 | reduce-window | flops 12484608 | bytes 786436 | tf_op jit(solution)/shard_map/reduce-window
  20.5 0.2 slice.10
  20.7 0.3 copy.23
  21.1 0.2 broadcast_add_fusion
  21.3 0.2 convert_reduce_fusion
  21.6 0.1 copy.20
  21.7 0.1 mul.51
  21.8 1.4 fusion.26
  23.2 1.3 fusion.27
  24.5 16.3 %scatter_custom_fusion = bf16[3072,2048]{1,0:T(8,128)(2,1)} fusion(s32[1536]{0:T(1024)S(1)} %fusion.33, bf16[]{:T(256)} %constant.8.clone.1, bf16[192,2048]{1,0:T(8,128)(2,1)S(1)} %fusion.27), kind=kCustom, calls=%fused_computation.19 | custom fusion | bytes 13369346 | tf_op jit(solution)/shard_map/scatter | solution.py:54
  40.9 149.1 %all_to_all.10 = bf16[32,2,48,2048]{3,2,1,0:T(8,128)(2,1)S(1)} all-to-all(bf16[32,2,48,2048]{3,2,1,0:T(8,128)(2,1)} %bitcast.78), channel_id=1, replica_groups=mesh['section'=4,'dp'=2,'expert'=16] {'dp','expert'}, dimensions={0} | all-to-all | bytes 25165824 | tf_op jit(solution)/shard_map/all_to_all | solution.py:57
  189.9 4.5 copy-done
  194.4 14.1 %fusion.1 = f32[2,32,48,768]{3,2,1,0:T(8,128)} fusion(bf16[32,2,48,2048]{3,2,1,0:T(8,128)(2,1)S(1)} %all_to_all.10, bf16[1,2,2048,768]{3,2,1,0:T(8,128)(2,1)} %param.10), kind=kOutput, calls=%fused_computation.5 | convolution fusion | flops 9663676416 | bytes 28311552 | tf_op jit(solution)/shard_map/secd,edf->secf/dot_general | solution.py:20
  208.4 29.3 %convert_bitcast_fusion = bf16[32,2,48,2048]{3,2,0,1:T(8,128)(2,1)} fusion(bf16[1,2,768,2048]{3,2,1,0:T(8,128)(2,1)} %param.11, f32[2,32,48,768]{3,2,1,0:T(8,128)} %fusion.1, bf16[32,2,48,2048]{3,2,1,0:T(8,128)(2,1)} %copy-done, bf16[1,2,2048,768]{3,2,1,0:T(8,128)(2,1)} %param.9), kind=kOutput, calls=%fused_computation.4 | convolution fusion | flops 19347800064 | bytes 47185920 | tf_op jit(solution)/shard_map/secf,efd->secd/dot_general | solution.py:22
  237.8 10.8 %copy.27 = bf16[32,2,48,2048]{3,2,1,0:T(8,128)(2,1)} copy(bf16[32,2,48,2048]{3,2,0,1:T(8,128)(2,1)} %convert_bitcast_fusion) | data formatting | bytes 25165824 | tf_op jit(solution)/shard_map/convert_element_type | solution.py:22
  248.6 5.4 %all-to-all-start.1 = ((bf16[32,2,48,2048]{3,2,1,0:T(8,128)(2,1)}), bf16[32,2,48,2048]{3,2,1,0:T(8,128)(2,1)}, u32[]{:S(2)}, u32[]{:S(2)}) async-start(bf16[32,2,48,2048]{3,2,1,0:T(8,128)(2,1)} %copy.27), calls=%async_computation.1 | async-start | bytes 25165824 | tf_op jit(solution)/shard_map/all_to_all | solution.py:59
  254.1 0.1 copy.19
  254.2 194.4 %all-to-all-done.1 = bf16[32,2,48,2048]{3,2,1,0:T(8,128)(2,1)} async-done(((bf16[32,2,48,2048]{3,2,1,0:T(8,128)(2,1)}), bf16[32,2,48,2048]{3,2,1,0:T(8,128)(2,1)}, u32[]{:S(2)}, u32[]{:S(2)}) %all-to-all-start.1) | async-done | bytes 12582944 | tf_op jit(solution)/shard_map/all_to_all | solution.py:59
  448.6 19.0 %gather_fusion = bf16[1536,2048]{1,0:T(8,128)(2,1)} fusion(bf16[3072,2048]{1,0:T(8,128)(2,1)} %bitcast.19, s32[2048]{0:T(1024)S(1)} %pad_clamp_fusion), kind=kCustom, calls=%fused_computation | custom fusion | bytes 12589056 | tf_op jit(solution)/shard_map/gather | solution.py:60
  467.6 9.2 %fusion = f32[192,2048]{1,0:T(8,128)S(1)} fusion(bf16[1536,2048]{1,0:T(8,128)(2,1)} %gather_fusion, f32[192,8]{1,0:T(8,128)S(1)} %copy.19), kind=kLoop, calls=%fused_computation.3 | loop fusion | flops 9043968 | bytes 7870464 | tf_op jit(solution)/shard_map/reduce_sum | solution.py:63
  476.9 0.2 fusion.28
  477.1 1.7 collective-permute-start
  478.7 0.1 copy.28
  478.9 0.1 div.46
  479.2 0.4 convolution_bitcast_fusion
  479.6 2.5 all-reduce.1
  482.1 46.1 %all-reduce = (f32[64]{0:T(128)S(1)}, f32[64]{0:T(128)S(1)}) all-reduce(f32[64]{0:T(128)S(1)} %get-tuple-element.6, f32[64]{0:T(128)S(1)} %get-tuple-element.7), channel_id=1, replica_groups=mesh['section'=4,'dp'=2,'expert'=16] {'expert'}, use_global_device_ids=true, to_apply=%region_11.12 | all-reduce | flops 128 | bytes 1024 | tf_op jit(solution)/shard_map/psum | solution.py:9
  528.2 0.6 multiply_reduce_fusion
  529.5 0.9 copy.44
  (21 shorter events, 0.6 us)
Async XLA Ops:
  189.9 4.5 copy-start
  248.6 5.5 %copy-start.2 = (f32[1,192,8]{1,2,0:T(8,128)S(1)}, f32[1,192,8]{1,2,0:T(8,128)}, u32[]{:S(2)}) copy-start(f32[1,192,8]{1,2,0:T(8,128)} %param.8) | copy-start | bytes 18436
  248.6 200.0 %all-to-all-start.1 = ((bf16[32,2,48,2048]{3,2,1,0:T(8,128)(2,1)}), bf16[32,2,48,2048]{3,2,1,0:T(8,128)(2,1)}, u32[]{:S(2)}, u32[]{:S(2)}) async-start(bf16[32,2,48,2048]{3,2,1,0:T(8,128)(2,1)} %copy.27), calls=%async_computation.1 | async-start | bytes 25165824 | tf_op jit(solution)/shard_map/all_to_all | solution.py:59
  448.6 28.2 %copy-start.1 = (bf16[1,192,2048]{2,1,0:T(8,128)(2,1)S(1)}, bf16[1,192,2048]{2,1,0:T(8,128)(2,1)}, u32[]{:S(2)}) copy-start(bf16[1,192,2048]{2,1,0:T(8,128)(2,1)} %param.6) | copy-start | bytes 2359300
  477.1 52.4 %collective-permute-start = (bf16[192,2048]{1,0:T(8,128)(2,1)S(1)}, bf16[192,2048]{1,0:T(8,128)(2,1)S(1)}, u32[]{:S(2)}, u32[]{:S(2)}) collective-permute-start(bf16[192,2048]{1,0:T(8,128)(2,1)S(1)} %fusion.28), channel_id=1, source_target_pairs={{0,32},{32,64},{64,96},{96,0},{1,33},{33,65},{65,97},{97,1},{2,34}... | collective-permute-start | bytes 2359304 | tf_op jit(solution)/shard_map/ppermute | solution.py:15
